TPU v7x, 32 devices: a whole 2x2x4 slice. The times are simulated.
32 devices in a mesh: heads: 4 (over y, x), seq: 8 (over z, core).
Axes of the slice: x: 2, y: 2, z: 4, core: 2. Of those that a mesh axis runs over, the one named last changes fastest.
Arguments:
- local_qkv: bfloat16 [3, 4096, 2048], P(None, 'seq', 'heads'), may hold values from -8 to 8
- routed_qkv: bfloat16 [3, 4096, 2048], P(None, 'seq', 'heads'), may hold values from -8 to 8
- clusters: int32 [16, 4096], P('heads', 'seq'), may hold values from 0 to 127, as said below
- wo_local: bfloat16 [2048, 4096], P('heads'), may hold values from -0.5 to 0.5
- wo_routed: bfloat16 [2048, 4096], P('heads'), may hold values from -0.5 to 0.5
Outputs:
- layer_out: bfloat16 [4096, 4096], P('seq', 'heads')
Inputs may be any that keep to these rules, and one draw needn't show every extreme that they name: `clusters`: in every routed head, no cluster holds more than 8 of the 512 tokens of one aligned block of tokens; in every head and block some cluster holds exactly 8 of them.
All inputs are finite; a program needn't handle non-finite values.
Results may differ from a plain program's by a relative error of at most 0.009.
Values may be sent and summed in bfloat16 or wider, within the bound.
A program may use at most 128 MiB of HBM per device.

v0:
```python
import jax
import jax.numpy as jnp
from jax import lax
from jax.sharding import PartitionSpec as P

DH = 128
WINDOW = 512
NCLUST = 128
masked_fill = -1e30


def passed_along(block, axis, distance):
    devices = range(lax.axis_size(axis))
    route = [(i - distance, i) for i in devices if i - distance in devices]
    return lax.ppermute(block, axis, route)


def soft_weights(scores, allowed):
    scores = jnp.where(allowed, scores, masked_fill)
    top_score = jnp.max(scores, axis=-1, keepdims=True)
    raised = jnp.exp(scores - top_score)
    return (raised / jnp.sum(raised, axis=-1, keepdims=True)).astype(jnp.bfloat16)


def window_part(local_qkv):
    tok_count = local_qkv.shape[1]
    width = local_qkv.shape[2]
    head_count = width // DH
    seq_index = lax.axis_index("seq")
    earlier = passed_along(local_qkv[1:], "seq", 1)
    joined = jnp.concatenate([earlier, local_qkv[1:]], axis=1)
    queries = local_qkv[0].reshape(tok_count, head_count, DH)
    keys_all = joined[0].reshape(2 * tok_count, head_count, DH)
    values_all = joined[1].reshape(2 * tok_count, head_count, DH)

    def one_block(index):
        start = index * WINDOW
        scores = jnp.einsum(
            "qhd,khd->hqk", queries, keys_all, preferred_element_type=jnp.float32
        ) * DH ** (-0.5)
        query_at = start + jnp.arange(WINDOW, dtype=jnp.int32)
        key_index = tok_count + start - WINDOW + jnp.arange(2 * WINDOW, dtype=jnp.int32)
        offset = (key_index - tok_count)[None, :] - query_at[:, None]
        present = (seq_index > 0) | (key_index >= tok_count)
        allowed = (offset <= 0) & (offset > -WINDOW) & present[None, :]
        weights = soft_weights(scores, allowed[None])
        result = jnp.einsum("hqk,khd->qhd", weights, values_all, preferred_element_type=jnp.float32)
        return result.astype(jnp.bfloat16).reshape(WINDOW, width)

    blocks = lax.map(one_block, jnp.arange(tok_count // WINDOW, dtype=jnp.int32))
    return blocks.reshape(tok_count, width)


def routed_part(routed_qkv, clusters):
    tok_count = routed_qkv.shape[1]
    head_count = clusters.shape[0]
    seq_count = lax.axis_size("seq")
    seq_index = lax.axis_index("seq")
    most_rows = 2 * tok_count // NCLUST
    slot_total = NCLUST * most_rows
    per_owner = slot_total // seq_count
    onehot = (clusters[:, :, None] == jnp.arange(NCLUST, dtype=jnp.int32)[None, None, :]).astype(
        jnp.int32
    )
    before = jnp.cumsum(onehot, axis=1) - onehot
    rank_index = jnp.sum(before * onehot, axis=-1)
    slot_index = clusters * most_rows + rank_index
    head_index = jnp.broadcast_to(
        jnp.arange(head_count, dtype=jnp.int32)[:, None], (head_count, tok_count)
    )
    token_ids = jnp.broadcast_to(
        jnp.arange(tok_count, dtype=jnp.int32)[None, :], (head_count, tok_count)
    )
    token_at = (
        jnp.full((head_count, slot_total), -1, jnp.int32).at[head_index, slot_index].set(token_ids)
    )
    row_data = (
        routed_qkv.reshape(3, tok_count, head_count, DH)
        .transpose(2, 1, 0, 3)
        .reshape(head_count, tok_count, 3 * DH)
    )
    picked = jnp.take_along_axis(row_data, jnp.maximum(token_at, 0)[:, :, None], axis=1)
    picked = jnp.where(token_at[:, :, None] >= 0, picked, jnp.zeros_like(picked))
    positions = jnp.where(token_at >= 0, seq_index * tok_count + token_at, -1)
    send_rows = picked.reshape(head_count, seq_count, per_owner, 3 * DH)
    send_places = positions.reshape(head_count, seq_count, per_owner)
    rows_in = lax.all_to_all(send_rows, "seq", split_axis=1, concat_axis=1, tiled=True)
    places_in = lax.all_to_all(send_places, "seq", split_axis=1, concat_axis=1, tiled=True)
    item_count = rows_in.shape[0]
    owned = per_owner // most_rows
    members = seq_count * most_rows
    grouped = rows_in.reshape(item_count, seq_count, owned, most_rows, 3 * DH).transpose(
        0, 2, 1, 3, 4
    )
    grouped = grouped.reshape(item_count, owned, members, 3 * DH)
    places = places_in.reshape(item_count, seq_count, owned, most_rows).transpose(0, 2, 1, 3)
    places = places.reshape(item_count, owned, members)
    scores = jnp.einsum(
        "ncqd,nckd->ncqk",
        grouped[..., :DH],
        grouped[..., DH : 2 * DH],
        preferred_element_type=jnp.float32,
    ) * DH ** (-0.5)
    allowed = (places[:, :, None, :] >= 0) & (places[:, :, None, :] <= places[:, :, :, None])
    weights = soft_weights(scores, allowed)
    result = jnp.einsum(
        "ncqk,nckd->ncqd", weights, grouped[..., 2 * DH :], preferred_element_type=jnp.float32
    )
    result = (
        result.astype(jnp.bfloat16)
        .reshape(item_count, owned, seq_count, most_rows, DH)
        .transpose(0, 2, 1, 3, 4)
    )
    result = result.reshape(item_count, seq_count, per_owner, DH)
    returned = lax.all_to_all(result, "seq", split_axis=1, concat_axis=1, tiled=True)
    returned = returned.reshape(head_count, slot_total, DH)
    mine = jnp.take_along_axis(returned, slot_index[:, :, None], axis=1)
    return mine.transpose(1, 0, 2).reshape(tok_count, head_count * DH)


def body(local_qkv, routed_qkv, clusters, wo_local, wo_routed):
    local_out = window_part(local_qkv)
    routed_out = routed_part(routed_qkv, clusters)
    group_sum = jnp.dot(local_out, wo_local, preferred_element_type=jnp.float32)
    group_sum = group_sum + jnp.dot(routed_out, wo_routed, preferred_element_type=jnp.float32)
    summed = lax.psum_scatter(
        group_sum.astype(jnp.bfloat16), "heads", scatter_dimension=1, tiled=True
    )
    return summed


def solution(mesh):
    return jax.shard_map(
        body,
        mesh=mesh,
        in_specs=(
            P(None, "seq", "heads"),
            P(None, "seq", "heads"),
            P("heads", "seq"),
            P("heads", None),
            P("heads", None),
        ),
        out_specs=P("seq", "heads"),
        check_vma=False,
    )
```

profile of v0, /device:TPU:0, one launch (start us, length us, event | category | flops | bytes accessed | tf_op | source)
XLA Modules:
  0.0 282.5 jit_solution(4169439975950401828)
XLA Ops:
  6.5 0.7 eq.26
  7.3 0.1 copy.73
  7.4 0.9 fusion.21
  8.3 0.0 copy-start.5
  8.3 0.2 broadcast_add_fusion
  8.5 0.0 copy-start.7
  8.5 0.0 copy-start.6
  8.6 0.0 copy-start.2
  8.6 0.1 copy.74
  8.7 0.3 copy-done.5
  9.0 0.6 fusion.19
  9.7 0.0 copy-done.7
  9.7 0.1 and_reduce_fusion
  9.8 0.0 copy-done.6
  9.8 0.1 multiply_reduce_fusion
  9.9 8.1 %scatter_custom_fusion = s32[4096]{0:T(1024)S(1)} fusion(s32[2048]{0:T(1024)S(1)} %bitcast.109, s32[2048]{0:T(1024)S(1)} %bitcast.108, s32[]{:T(128)} %constant.87.clone.1), kind=kCustom, calls=%fused_computation.62 | custom fusion | bytes 16388
  18.0 0.6 copy.75
  18.6 6.3 %all-to-all-start = ((s32[4,8,128]{2,0,1:T(4,128)}), s32[4,8,128]{2,0,1:T(4,128)S(1)}, u32[]{:S(2)}, u32[]{:S(2)}) async-start(s32[4,8,128]{2,0,1:T(4,128)} %copy.75), calls=%async_computation | async-start | bytes 32768 | tf_op jit(solution)/shard_map/all_to_all | solution.py:88
  25.0 0.0 copy-done.2
  25.0 0.7 copy.83
  25.7 0.1 copy.84
  25.8 0.9 copy.85
  26.7 44.7 %gather_fusion = bf16[4096,384]{1,0:T(8,128)(2,1)} fusion(bf16[4,512,384]{2,1,0:T(8,128)(2,1)S(1)} %copy.85, s32[4096]{0:T(1024)S(1)} %bitcast.93), kind=kCustom, calls=%fused_computation | custom fusion | bytes 6324224 | tf_op jit(solution)/shard_map/jit(take_along_axis)/gather | solution.py:82
  71.5 4.8 %fusion.7 = bf16[4,8,128,384]{3,2,0,1:T(8,128)(2,1)} fusion(bf16[4,8,128,384]{3,2,1,0:T(8,128)(2,1)} %bitcast.96, pred[4,8,128]{2,0,1:T(4,128)(4,1)S(1)} %copy.82, pred[4,8,128]{2,0,1:T(4,128)(4,1)S(1)} %copy.81), kind=kLoop, calls=%fused_computation.16 | loop fusion | flops 3145728 | bytes 6299648 | tf_op jit(solution)/shard_map/jit(_where)/select_n | solution.py:83
  76.3 0.0 all-to-all-done
  76.3 5.1 %all-to-all-start.1 = ((bf16[4,8,128,384]{3,2,0,1:T(8,128)(2,1)}), bf16[4,8,128,384]{3,2,0,1:T(8,128)(2,1)S(1)}, u32[]{:S(2)}, u32[]{:S(2)}) async-start(bf16[4,8,128,384]{3,2,0,1:T(8,128)(2,1)} %fusion.7), calls=%async_computation.1 | async-start | bytes 6291456 | tf_op jit(solution)/shard_map/all_to_all | solution.py:87
  81.4 2.3 slice.28
  83.6 2.3 copy.99
  85.9 3.4 %collective-permute-start = (bf16[2,512,512]{1,2,0:T(8,128)(2,1)}, bf16[2,512,512]{1,2,0:T(8,128)(2,1)}, u32[]{:S(2)}, u32[]{:S(2)}) collective-permute-start(bf16[2,512,512]{1,2,0:T(8,128)(2,1)} %copy.99), channel_id=1, source_target_pairs={{0,1},{1,2},{2,3},{3,4},{4,5},{5,6},{6,7},{8,9},{9,10},{10,11},{11... | collective-permute-start | bytes 3145736 | tf_op jit(solution)/shard_map/ppermute | solution.py:15
  89.3 1.9 slice.31
  91.2 2.1 copy.100
  93.3 1.6 fusion.11
  94.9 0.2 reshape.152
  95.1 0.1 copy.77
  95.2 0.1 copy.79
  95.3 0.1 copy.78
  95.4 0.0 collective-permute-done
  95.4 3.2 %pad_maximum_fusion = (bf16[1,1024,512]{1,2,0:T(8,128)(2,1)}, bf16[1,1024,512]{1,2,0:T(8,128)(2,1)}) fusion(bf16[2,512,512]{1,2,0:T(8,128)(2,1)} %copy.99, bf16[2,512,512]{1,2,0:T(8,128)(2,1)} %collective-permute-done), kind=kLoop, calls=%fused_computation.34 | loop fusion | flops 4194304 | bytes 4194304 | tf_op jit(solution)/shard_map/concatenate | solution.py:31
  98.6 54.3 %all-to-all-done.1 = bf16[4,8,128,384]{3,2,0,1:T(8,128)(2,1)S(1)} async-done(((bf16[4,8,128,384]{3,2,0,1:T(8,128)(2,1)}), bf16[4,8,128,384]{3,2,0,1:T(8,128)(2,1)S(1)}, u32[]{:S(2)}, u32[]{:S(2)}) %all-to-all-start.1) | async-done | bytes 3145760 | tf_op jit(solution)/shard_map/all_to_all | solution.py:87
  152.9 0.6 copy_bitcast_fusion
  153.5 0.0 copy-start.1
  153.5 3.2 %multiply_select_fusion = f32[4,16,64,64]{2,3,1,0:T(8,128)S(1)} fusion(bf16[4,16,64,384]{3,2,1,0:T(8,128)(2,1)S(1)} %copy_bitcast_fusion, s32[4,16,64]{2,1,0:T(8,128)S(1)} %copy.79, pred[4,16,64]{2,1,0:T(8,128)(4,1)S(1)} %copy.78), kind=kOutput, calls=%fused_computation.21 | convolution fusion | flops 68157440 | bytes 3219456 | tf_op jit(solution)/shard_map/ncqd,nckd->ncqk/dot_general | solution.py:98
  156.7 0.0 copy-done.1
  156.7 0.5 fusion.35
  157.2 2.0 fusion.12
  159.2 0.3 copy.111
  159.5 0.0 copy-start.4
  159.5 1.0 copy.91
  160.6 16.2 %all-to-all-start.2 = ((bf16[4,8,128,128]{3,2,0,1:T(8,128)(2,1)}), bf16[4,8,128,128]{3,2,0,1:T(8,128)(2,1)S(1)}, u32[]{:S(2)}, u32[]{:S(2)}) async-start(bf16[4,8,128,128]{3,2,0,1:T(8,128)(2,1)} %copy.91), calls=%async_computation.2 | async-start | bytes 2097152 | tf_op jit(solution)/shard_map/all_to_all | solution.py:115
  176.7 0.2 reduce-scatter.2.cloned.1.call-start
  177.0 0.0 copy-done.4
  177.0 0.0 copy-start.3
  177.0 7.9 %fusion.34 = (f32[4,512]{1,0:T(4,128)S(1)}, f32[4,512,1024]{1,2,0:T(8,128)}) fusion(pred[512,1024]{0,1:T(8,128)(4,1)} %fusion.11, bf16[1024,4,128]{0,2,1:T(8,128)(2,1)S(1)} %bitcast.105, bf16[512,4,128]{0,2,1:T(8,128)(2,1)} %bitcast.107), kind=kOutput, calls=%fused_computation.74 | convolution fusion | flops 545260544 | bytes 10493952 | tf_op jit(solution)/shard_map/while/body/eval_jaxpr/sub | solution.py:21
  184.9 4.3 %fusion.13 = bf16[4,128,512]{2,1,0:T(8,128)(2,1)S(1)} fusion(bf16[1024,4,128]{0,2,1:T(8,128)(2,1)S(1)} %bitcast.104, f32[4,512,1024]{1,2,0:T(8,128)} %get-tuple-element.30, f32[4,512]{1,0:T(4,128)S(1)} %get-tuple-element.29), kind=kOutput, calls=%fused_computation.29 | convolution fusion | flops 541327360 | bytes 9969664 | tf_op jit(solution)/shard_map/while/body/eval_jaxpr/hqk,khd->qhd/dot_general | solution.py:47
  189.2 0.2 copy-done
  189.5 5.6 %fusion.36 = f32[512,4096]{1,0:T(8,128)} fusion(bf16[512,512]{0,1:T(8,128)(2,1)S(1)} %bitcast.106, bf16[512,4096]{1,0:T(8,128)(2,1)S(1)} %copy-done), kind=kOutput, calls=%fused_computation.76 | convolution fusion | flops 2147483648 | bytes 13107200 | tf_op jit(solution)/shard_map/dot_general | solution.py:124
  195.0 8.3 %all-to-all-done.2 = bf16[4,8,128,128]{3,2,0,1:T(8,128)(2,1)S(1)} async-done(((bf16[4,8,128,128]{3,2,0,1:T(8,128)(2,1)}), bf16[4,8,128,128]{3,2,0,1:T(8,128)(2,1)S(1)}, u32[]{:S(2)}, u32[]{:S(2)}) %all-to-all-start.2) | async-done | bytes 1048608 | tf_op jit(solution)/shard_map/all_to_all | solution.py:115
  203.3 0.1 copy.92
  203.4 11.1 %gather_fusion.1 = bf16[2048,128]{1,0:T(8,128)(2,1)S(1)} fusion(bf16[4,1024,128]{2,1,0:T(8,128)(2,1)S(1)} %bitcast.95, s32[2048]{0:T(1024)S(1)} %bitcast.94), kind=kCustom, calls=%fused_computation.1 | custom fusion | bytes 1064960 | tf_op jit(solution)/shard_map/jit(take_along_axis)/gather | solution.py:117
  214.6 0.2 copy.93
  214.8 0.1 bitcast_select_fusion.4
  214.9 9.0 %add_convert_fusion = bf16[512,4096]{1,0:T(8,128)(2,1)} fusion(f32[512,4096]{1,0:T(8,128)} %fusion.36, bf16[512,512]{0,1:T(8,128)(2,1)S(1)} %bitcast.100, bf16[512,4096]{1,0:T(8,128)(2,1)} %param.9), kind=kOutput, calls=%fused_computation.6 | convolution fusion | flops 2151677952 | bytes 17301504 | tf_op jit(solution)/shard_map/dot_general | solution.py:125
  223.9 0.0 reduce-scatter.2.cloned.1.call-update
  223.9 51.7 %reduce-scatter.2.cloned.1.call-done = bf16[512,1024]{1,0:T(8,128)(2,1)} async-done(((bf16[512,4096]{1,0:T(8,128)(2,1)}), bf16[512,1024]{1,0:T(8,128)(2,1)}) %reduce-scatter.2.cloned.1.call-update) | async-done | bytes 1048592 | tf_op jit(solution)/shard_map/reduce_scatter | solution.py:126
  (25 shorter events, 0.2 us)
Async XLA Ops:
  8.3 0.7 copy-start.5
  8.5 1.2 copy-start.7
  8.5 1.2 copy-start.6
  8.6 16.5 %copy-start.2 = (bf16[3,512,512]{2,1,0:T(8,128)(2,1)S(1)}, bf16[3,512,512]{2,1,0:T(8,128)(2,1)}, u32[]{:S(2)}) copy-start(bf16[3,512,512]{2,1,0:T(8,128)(2,1)} %param.6) | copy-start | bytes 4718596
  18.6 57.7 %all-to-all-start = ((s32[4,8,128]{2,0,1:T(4,128)}), s32[4,8,128]{2,0,1:T(4,128)S(1)}, u32[]{:S(2)}, u32[]{:S(2)}) async-start(s32[4,8,128]{2,0,1:T(4,128)} %copy.75), calls=%async_computation | async-start | bytes 32768 | tf_op jit(solution)/shard_map/all_to_all | solution.py:88
  76.3 76.6 %all-to-all-start.1 = ((bf16[4,8,128,384]{3,2,0,1:T(8,128)(2,1)}), bf16[4,8,128,384]{3,2,0,1:T(8,128)(2,1)S(1)}, u32[]{:S(2)}, u32[]{:S(2)}) async-start(bf16[4,8,128,384]{3,2,0,1:T(8,128)(2,1)} %fusion.7), calls=%async_computation.1 | async-start | bytes 6291456 | tf_op jit(solution)/shard_map/all_to_all | solution.py:87
  85.9 9.5 %collective-permute-start = (bf16[2,512,512]{1,2,0:T(8,128)(2,1)}, bf16[2,512,512]{1,2,0:T(8,128)(2,1)}, u32[]{:S(2)}, u32[]{:S(2)}) collective-permute-start(bf16[2,512,512]{1,2,0:T(8,128)(2,1)} %copy.99), channel_id=1, source_target_pairs={{0,1},{1,2},{2,3},{3,4},{4,5},{5,6},{6,7},{8,9},{9,10},{10,11},{11... | collective-permute-start | bytes 3145736 | tf_op jit(solution)/shard_map/ppermute | solution.py:15
  153.5 3.2 %copy-start.1 = (bf16[4,16,64,384]{3,2,1,0:T(8,128)(2,1)}, bf16[4,16,64,384]{3,2,1,0:T(8,128)(2,1)S(1)}, u32[]{:S(2)}) copy-start(bf16[4,16,64,384]{3,2,1,0:T(8,128)(2,1)S(1)} %copy_bitcast_fusion) | copy-start | bytes 9437188
  159.5 17.5 %copy-start.4 = (bf16[1,1024,512]{1,2,0:T(8,128)(2,1)S(1)}, bf16[1,1024,512]{1,2,0:T(8,128)(2,1)}, u32[]{:S(2)}) copy-start(bf16[1,1024,512]{1,2,0:T(8,128)(2,1)} %get-tuple-element.15) | copy-start | bytes 3145732
  160.6 42.8 %all-to-all-start.2 = ((bf16[4,8,128,128]{3,2,0,1:T(8,128)(2,1)}), bf16[4,8,128,128]{3,2,0,1:T(8,128)(2,1)S(1)}, u32[]{:S(2)}, u32[]{:S(2)}) async-start(bf16[4,8,128,128]{3,2,0,1:T(8,128)(2,1)} %copy.91), calls=%async_computation.2 | async-start | bytes 2097152 | tf_op jit(solution)/shard_map/all_to_all | solution.py:115
  176.7 98.9 %reduce-scatter.2.cloned.1.call-start = ((), (), s32[]{:S(2)}) async-start(), calls=%async_computation.4 | async-start | bytes 5242880 | tf_op jit(solution)/shard_map/reduce_scatter | solution.py:126
  177.0 7.9 %copy-start.3 = (bf16[1,1024,512]{1,2,0:T(8,128)(2,1)S(1)}, bf16[1,1024,512]{1,2,0:T(8,128)(2,1)}, u32[]{:S(2)}) copy-start(bf16[1,1024,512]{1,2,0:T(8,128)(2,1)} %get-tuple-element.16) | copy-start | bytes 3145732
  184.9 4.6 %copy-start = (bf16[512,4096]{1,0:T(8,128)(2,1)S(1)}, bf16[512,4096]{1,0:T(8,128)(2,1)}, u32[]{:S(2)}) copy-start(bf16[512,4096]{1,0:T(8,128)(2,1)} %param.8) | copy-start | bytes 12582916
Sparse Core Ops, SparseCore 0:
  224.0 51.5 reduce-scatter.1
where the time goes:
time: 283 us
  waiting for transfers between devices  114 us (40%)
  local copies, waits for them, and re-layouts  79 us (28%)
  matrix products  32 us (11%)
  starting transfers between devices  31.2 us (11%)
  between operations  13.8 us (5%)
  other arithmetic  12.2 us (4%)
    all_to_all x1, waiting for transfers between devices, routed_part(): lax.all_to_all(send_rows, 'seq', split_axis=1, concat_axis=1, tiled=True)  54.3 us
    reduce_scatter x1, waiting for transfers between devices, body(): lax.psum_scatter(group_sum.astype(jnp.bfloat16), 'heads', scatter_dimensi...  51.7 us
    gather x2, local copies, waits for them, and re-layouts, routed_part(): jnp.take_along_axis(row_data, jnp.maximum(token_at, 0)[:, :, None], axis=1)  44.8 us
    all_to_all x1, starting transfers between devices, routed_part(): lax.all_to_all(result, 'seq', split_axis=1, concat_axis=1, tiled=True)  16.2 us
    unnamed x25, local copies, waits for them, and re-layouts  13.7 us
    gather x2, local copies, waits for them, and re-layouts, routed_part(): mine = jnp.take_along_axis(returned, slot_index[:, :, None], axis=1)  11.3 us
    dot_general x1, matrix products, body(): jnp.dot(routed_out, wo_routed, preferred_element_type=jnp.float32)  9.04 us
    all_to_all x1, waiting for transfers between devices, routed_part(): lax.all_to_all(result, 'seq', split_axis=1, concat_axis=1, tiled=True)  8.28 us
  transfers between devices with their start and end apart: 5, of which 3 were waited for; matrix products, arithmetic and copies ran while one was open for 29% of the time, Pallas kernels for 0%

commit v1 on v0

--- a/solution.py
+++ b/solution.py
@@ -84,7 +84,19 @@
     positions = jnp.where(token_at >= 0, seq_index * tok_count + token_at, -1)
     send_rows = picked.reshape(head_count, seq_count, per_owner, 3 * DH)
     send_places = positions.reshape(head_count, seq_count, per_owner)
-    rows_in = lax.all_to_all(send_rows, "seq", split_axis=1, concat_axis=1, tiled=True)
+    ways, here = (lax.axis_size("seq"), lax.axis_index("seq"))
+    width_2 = send_rows.shape[1] // ways
+    dims = list(send_rows.shape)
+    dims[1] = width_2
+    height = dims[1]
+    dims[1] = height * ways
+    full = jnp.zeros(dims, send_rows.dtype)
+    for mask in range(ways):
+        part = lax.dynamic_slice_in_dim(send_rows, (here ^ mask) * width_2, width_2, axis=1)
+        if mask:
+            part = lax.ppermute(part, "seq", [(d, d ^ mask) for d in range(ways)])
+        full = lax.dynamic_update_slice_in_dim(full, part, (here ^ mask) * height, axis=1)
+    rows_in = full
     places_in = lax.all_to_all(send_places, "seq", split_axis=1, concat_axis=1, tiled=True)
     item_count = rows_in.shape[0]
     owned = per_owner // most_rows

time: 283 us -> 269 us (0.951)
  waiting for transfers between devices: 114 us -> 86.9 us
  local copies, waits for them, and re-layouts: 79 us -> 87.9 us
  starting transfers between devices: 31.2 us -> 37.3 us
    all_to_all x1 -> x0, waiting for transfers between devices: 54.3 us -> none  [routed_part(): lax.all_to_all(send_rows, 'seq', split_axis=1, concat_axis=1, tiled=True)]
    all_to_all x1, waiting for transfers between devices: 0.01 us -> 19.8 us  [routed_part(): lax.all_to_all(send_places, 'seq', split_axis=1, concat_axis=1, tiled=True)]
    ppermute x0 -> x7, starting transfers between devices: none -> 9.68 us  [routed_part(): part = lax.ppermute(part, 'seq', [(d, d ^ mask) for d in range(ways)])]
    ppermute x0 -> x7, waiting for transfers between devices: none -> 9.66 us  [routed_part(): part = lax.ppermute(part, 'seq', [(d, d ^ mask) for d in range(ways)])]
    dynamic_update_slice x0 -> x7, local copies, waits for them, and re-layouts: none -> 5.43 us  [routed_part(): lax.dynamic_update_slice_in_dim(full, part, (here ^ mask) * height, axis=1)]
    all_to_all x1 -> x0, starting transfers between devices: 5.1 us -> none  [routed_part(): lax.all_to_all(send_rows, 'seq', split_axis=1, concat_axis=1, tiled=True)]
    all_to_all x1, starting transfers between devices: 16.2 us -> 19.3 us  [routed_part(): lax.all_to_all(result, 'seq', split_axis=1, concat_axis=1, tiled=True)]
    unnamed x25 -> x23, local copies, waits for them, and re-layouts: 13.7 us -> 15 us
  transfers between devices with their start and end apart: 5 -> 11, of which waited for: 3 -> 5; matrix products, arithmetic and copies ran while one was open for 29% -> 17% of each run, Pallas kernels for 0% -> 0%
where the time goes in v1:
time: 269 us; the launch traced here: 268 us
  local copies, waits for them, and re-layouts  87.9 us (33%)
  waiting for transfers between devices  86.9 us (32%)
  starting transfers between devices  37.3 us (14%)
  matrix products  32.1 us (12%)
  between operations  13.8 us (5%)
  other arithmetic  9.93 us (4%)
    reduce_scatter x1, waiting for transfers between devices, body(): lax.psum_scatter(group_sum.astype(jnp.bfloat16), 'heads', scatter_dimensi...  51.7 us
    gather x2, local copies, waits for them, and re-layouts, routed_part(): jnp.take_along_axis(row_data, jnp.maximum(token_at, 0)[:, :, None], axis=1)  44.7 us
    all_to_all x1, waiting for transfers between devices, routed_part(): lax.all_to_all(send_places, 'seq', split_axis=1, concat_axis=1, tiled=True)  19.8 us
    all_to_all x1, starting transfers between devices, routed_part(): lax.all_to_all(result, 'seq', split_axis=1, concat_axis=1, tiled=True)  19.3 us
    unnamed x23, local copies, waits for them, and re-layouts  15 us
    gather x2, local copies, waits for them, and re-layouts, routed_part(): mine = jnp.take_along_axis(returned, slot_index[:, :, None], axis=1)  11.3 us
    ppermute x7, starting transfers between devices, routed_part(): part = lax.ppermute(part, 'seq', [(d, d ^ mask) for d in range(ways)])  9.68 us
    ppermute x7, waiting for transfers between devices, routed_part(): part = lax.ppermute(part, 'seq', [(d, d ^ mask) for d in range(ways)])  9.66 us
  transfers between devices with their start and end apart: 11, of which 5 were waited for; matrix products, arithmetic and copies ran while one was open for 17% of the time, Pallas kernels for 0%

profile of v1, /device:TPU:0, one launch (start us, length us, event | category | flops | bytes accessed | tf_op | source)
XLA Modules:
  0.0 268.1 jit_solution(4236204611974657427)
XLA Ops:
  6.5 0.8 eq.26
  7.3 0.1 copy.71
  7.5 0.9 fusion.20
  8.4 0.2 broadcast_add_fusion
  8.6 0.1 copy.72
  8.8 0.6 fusion.18
  9.4 0.1 multiply_reduce_fusion
  9.5 0.1 and_reduce_fusion
  9.6 8.1 %scatter_custom_fusion = s32[4096]{0:T(1024)S(1)} fusion(s32[2048]{0:T(1024)S(1)} %bitcast.107, s32[2048]{0:T(1024)S(1)} %bitcast.108, s32[]{:T(128)} %constant.58.clone.1), kind=kCustom, calls=%fused_computation.62 | custom fusion | bytes 16388
  17.8 0.7 copy.79
  18.5 0.1 copy.80
  18.6 0.9 copy.81
  19.5 44.7 %gather_fusion = bf16[4096,384]{1,0:T(8,128)(2,1)} fusion(bf16[4,512,384]{2,1,0:T(8,128)(2,1)S(1)} %copy.81, s32[4096]{0:T(1024)S(1)} %bitcast.92), kind=kCustom, calls=%fused_computation | custom fusion | bytes 6324224 | tf_op jit(solution)/shard_map/jit(take_along_axis)/gather | solution.py:82
  64.2 3.4 %select_select_fusion = bf16[4,8,128,384]{3,2,1,0:T(8,128)(2,1)S(1)} fusion(bf16[4,8,128,384]{3,2,1,0:T(8,128)(2,1)} %bitcast.95, pred[4,8,128]{2,1,0:T(8,128)(4,1)S(1)} %get-tuple-element.36, pred[4,8,128]{2,1,0:T(8,128)(4,1)S(1)} %get-tuple-element.35), kind=kLoop, calls=%fused_computation.15 | loop fusion | flops 3145728 | bytes 6299648 | tf_op jit(solution)/shard_map/jit(_where)/select_n | solution.py:83
  67.6 0.5 broadcast_in_dim.106
  68.1 1.6 constant_dynamic-slice_fusion
  69.7 0.5 collective-permute-start.1
  70.1 2.6 collective-permute-start.2
  72.7 0.1 collective-permute-start.3
  72.9 2.7 %collective-permute-start.4 = (bf16[4,1,128,384]{3,2,1,0:T(8,128)(2,1)}, bf16[4,1,128,384]{3,2,1,0:T(8,128)(2,1)}, u32[]{:S(2)}, u32[]{:S(2)}) collective-permute-start(bf16[4,1,128,384]{3,2,1,0:T(8,128)(2,1)} %get-tuple-element.24), channel_id=1, source_target_pairs={{0,4},{1,5},{2,6},{3,7},{4,0},{5,1},{6,2},{7,3},{8,12},{9,13},{10,... | collective-permute-start | bytes 1179656 | tf_op jit(solution)/shard_map/ppermute | solution.py:97
  75.6 0.6 copy.73
  76.2 4.9 %all-to-all-start = ((s32[4,8,128]{2,0,1:T(4,128)}), s32[4,8,128]{2,0,1:T(4,128)S(1)}, u32[]{:S(2)}, u32[]{:S(2)}) async-start(s32[4,8,128]{2,0,1:T(4,128)} %copy.73), calls=%async_computation | async-start | bytes 32768 | tf_op jit(solution)/shard_map/all_to_all | solution.py:100
  81.2 1.6 fusion.10
  82.8 2.3 slice.28
  85.1 1.9 slice.31
  86.9 2.3 copy.92
  89.2 2.0 copy.93
  91.3 19.8 %all-to-all-done = s32[4,8,128]{2,0,1:T(4,128)S(1)} async-done(((s32[4,8,128]{2,0,1:T(4,128)}), s32[4,8,128]{2,0,1:T(4,128)S(1)}, u32[]{:S(2)}, u32[]{:S(2)}) %all-to-all-start) | async-done | bytes 16416 | tf_op jit(solution)/shard_map/all_to_all | solution.py:100
  111.0 0.2 reshape.152
  111.2 0.1 copy.75
  111.4 0.1 copy.76
  111.4 0.1 copy.77
  111.5 3.7 %collective-permute-start.6 = (bf16[4,1,128,384]{3,2,1,0:T(8,128)(2,1)}, bf16[4,1,128,384]{3,2,1,0:T(8,128)(2,1)S(1)}, u32[]{:S(2)}, u32[]{:S(2)}) collective-permute-start(bf16[4,1,128,384]{3,2,1,0:T(8,128)(2,1)} %get-tuple-element.16), channel_id=1, source_target_pairs={{0,6},{1,7},{2,4},{3,5},{4,2},{5,3},{6,0},{7,1},{8,14},{9,15},{10,... | collective-permute-start | bytes 1179656 | tf_op jit(solution)/shard_map/ppermute | solution.py:97
  115.3 1.1 constant_dynamic-update-slice_fusion.6
  116.3 0.1 collective-permute-start.7
  116.4 1.1 constant_dynamic-update-slice_fusion.5
  117.5 3.2 %collective-permute-start = (bf16[2,512,512]{1,2,0:T(8,128)(2,1)}, bf16[2,512,512]{1,2,0:T(8,128)(2,1)}, u32[]{:S(2)}, u32[]{:S(2)}) collective-permute-start(bf16[2,512,512]{1,2,0:T(8,128)(2,1)} %copy.92), channel_id=1, source_target_pairs={{0,1},{1,2},{2,3},{3,4},{4,5},{5,6},{6,7},{8,9},{9,10},{10,11},{11... | collective-permute-start | bytes 3145736 | tf_op jit(solution)/shard_map/ppermute | solution.py:15
  120.6 1.1 constant_dynamic-update-slice_fusion.4
  121.7 1.1 constant_dynamic-update-slice_fusion.3
  122.8 1.1 constant_dynamic-update-slice_fusion.2
  123.8 1.8 collective-permute-done.6
  125.6 0.1 constant_dynamic-update-slice_fusion.1
  125.7 7.8 %collective-permute-done.7 = bf16[4,1,128,384]{3,2,1,0:T(8,128)(2,1)S(1)} collective-permute-done((bf16[4,1,128,384]{3,2,1,0:T(8,128)(2,1)}, bf16[4,1,128,384]{3,2,1,0:T(8,128)(2,1)S(1)}, u32[]{:S(2)}, u32[]{:S(2)}) %collective-permute-start.7) | collective-permute-done | bytes 393248 | tf_op jit(solution)/shard_map/ppermute | solution.py:97
  133.6 0.1 constant_dynamic-update-slice_fusion
  133.6 0.6 copy_bitcast_fusion
  134.2 1.7 copy-done.2
  135.9 3.1 %multiply_select_fusion = f32[4,16,64,64]{2,3,1,0:T(8,128)S(1)} fusion(bf16[4,16,64,384]{3,2,1,0:T(8,128)(2,1)S(1)} %copy_bitcast_fusion, s32[4,16,64]{2,1,0:T(8,128)S(1)} %copy.77, pred[4,16,64]{2,1,0:T(8,128)(4,1)S(1)} %copy.76), kind=kOutput, calls=%fused_computation.20 | convolution fusion | flops 68157440 | bytes 3219456 | tf_op jit(solution)/shard_map/ncqd,nckd->ncqk/dot_general | solution.py:110
  139.0 0.5 fusion.34
  139.5 2.0 fusion.11
  141.5 0.3 copy.101
  141.8 1.1 copy.85
  142.9 19.3 %all-to-all-start.1 = ((bf16[4,8,128,128]{3,2,0,1:T(8,128)(2,1)}), bf16[4,8,128,128]{3,2,0,1:T(8,128)(2,1)S(1)}, u32[]{:S(2)}, u32[]{:S(2)}) async-start(bf16[4,8,128,128]{3,2,0,1:T(8,128)(2,1)} %copy.85), calls=%async_computation.1 | async-start | bytes 2097152 | tf_op jit(solution)/shard_map/all_to_all | solution.py:127
  162.3 0.2 reduce-scatter.2.cloned.1.call-start
  162.5 2.3 pad_maximum_fusion
  164.9 8.1 %fusion.33 = (f32[4,512]{1,0:T(4,128)S(1)}, f32[4,512,1024]{1,2,0:T(8,128)}) fusion(pred[512,1024]{0,1:T(8,128)(4,1)} %fusion.10, bf16[1024,4,128]{0,2,1:T(8,128)(2,1)} %bitcast.104, bf16[512,4,128]{0,2,1:T(8,128)(2,1)} %bitcast.106), kind=kOutput, calls=%fused_computation.88 | convolution fusion | flops 545260544 | bytes 10493952 | tf_op jit(solution)/shard_map/while/body/eval_jaxpr/sub | solution.py:21
  173.0 4.3 %fusion.12 = bf16[4,128,512]{2,1,0:T(8,128)(2,1)S(1)} fusion(bf16[1024,4,128]{0,2,1:T(8,128)(2,1)S(1)} %bitcast.103, f32[4,512,1024]{1,2,0:T(8,128)} %get-tuple-element.38, f32[4,512]{1,0:T(4,128)S(1)} %get-tuple-element.37), kind=kOutput, calls=%fused_computation.28 | convolution fusion | flops 541327360 | bytes 9969664 | tf_op jit(solution)/shard_map/while/body/eval_jaxpr/hqk,khd->qhd/dot_general | solution.py:47
  177.3 0.2 copy-done
  177.5 5.6 %fusion.35 = f32[512,4096]{1,0:T(8,128)} fusion(bf16[512,512]{0,1:T(8,128)(2,1)S(1)} %bitcast.105, bf16[512,4096]{1,0:T(8,128)(2,1)S(1)} %copy-done), kind=kOutput, calls=%fused_computation.90 | convolution fusion | flops 2147483648 | bytes 13107200 | tf_op jit(solution)/shard_map/dot_general | solution.py:136
  183.1 5.7 %all-to-all-done.1 = bf16[4,8,128,128]{3,2,0,1:T(8,128)(2,1)S(1)} async-done(((bf16[4,8,128,128]{3,2,0,1:T(8,128)(2,1)}), bf16[4,8,128,128]{3,2,0,1:T(8,128)(2,1)S(1)}, u32[]{:S(2)}, u32[]{:S(2)}) %all-to-all-start.1) | async-done | bytes 1048608 | tf_op jit(solution)/shard_map/all_to_all | solution.py:127
  188.9 0.1 copy.86
  189.0 11.1 %gather_fusion.1 = bf16[2048,128]{1,0:T(8,128)(2,1)S(1)} fusion(bf16[4,1024,128]{2,1,0:T(8,128)(2,1)S(1)} %bitcast.94, s32[2048]{0:T(1024)S(1)} %bitcast.93), kind=kCustom, calls=%fused_computation.1 | custom fusion | bytes 1064960 | tf_op jit(solution)/shard_map/jit(take_along_axis)/gather | solution.py:129
  200.1 0.2 copy.87
  200.4 9.0 %add_convert_fusion = bf16[512,4096]{1,0:T(8,128)(2,1)} fusion(f32[512,4096]{1,0:T(8,128)} %fusion.35, bf16[512,512]{0,1:T(8,128)(2,1)S(1)} %bitcast.99, bf16[512,4096]{1,0:T(8,128)(2,1)} %param.9), kind=kOutput, calls=%fused_computation.6 | convolution fusion | flops 2151677952 | bytes 17301504 | tf_op jit(solution)/shard_map/dot_general | solution.py:137
  209.5 51.7 %reduce-scatter.2.cloned.1.call-done = bf16[512,1024]{1,0:T(8,128)(2,1)} async-done(((bf16[512,4096]{1,0:T(8,128)(2,1)}), bf16[512,1024]{1,0:T(8,128)(2,1)}) %reduce-scatter.2.cloned.1.call-update) | async-done | bytes 1048592 | tf_op jit(solution)/shard_map/reduce_scatter | solution.py:138
  (42 shorter events, 0.3 us)
Async XLA Ops:
  6.5 2.2 copy-start.4
  7.5 2.0 copy-start.6
  7.5 2.0 copy-start.5
  8.4 9.4 %copy-start.3 = (bf16[3,512,512]{2,1,0:T(8,128)(2,1)S(1)}, bf16[3,512,512]{2,1,0:T(8,128)(2,1)}, u32[]{:S(2)}) copy-start(bf16[3,512,512]{2,1,0:T(8,128)(2,1)} %param.6) | copy-start | bytes 4718596
  69.7 41.9 %collective-permute-start.1 = (bf16[4,1,128,384]{3,2,1,0:T(8,128)(2,1)}, bf16[4,1,128,384]{3,2,1,0:T(8,128)(2,1)}, u32[]{:S(2)}, u32[]{:S(2)}) collective-permute-start(bf16[4,1,128,384]{3,2,1,0:T(8,128)(2,1)} %get-tuple-element.29), channel_id=1, source_target_pairs={{0,1},{1,0},{2,3},{3,2},{4,5},{5,4},{6,7},{7,6},{8,9},{9,8},{10,11... | collective-permute-start | bytes 1179656 | tf_op jit(solution)/shard_map/ppermute | solution.py:97
  70.1 46.2 %collective-permute-start.2 = (bf16[4,1,128,384]{3,2,1,0:T(8,128)(2,1)}, bf16[4,1,128,384]{3,2,1,0:T(8,128)(2,1)}, u32[]{:S(2)}, u32[]{:S(2)}) collective-permute-start(bf16[4,1,128,384]{3,2,1,0:T(8,128)(2,1)} %get-tuple-element.28), channel_id=1, source_target_pairs={{0,2},{1,3},{2,0},{3,1},{4,6},{5,7},{6,4},{7,5},{8,10},{9,11},{10,... | collective-permute-start | bytes 1179656 | tf_op jit(solution)/shard_map/ppermute | solution.py:97
  72.7 44.8 %collective-permute-start.3 = (bf16[4,1,128,384]{3,2,1,0:T(8,128)(2,1)}, bf16[4,1,128,384]{3,2,1,0:T(8,128)(2,1)}, u32[]{:S(2)}, u32[]{:S(2)}) collective-permute-start(bf16[4,1,128,384]{3,2,1,0:T(8,128)(2,1)} %get-tuple-element.26), channel_id=1, source_target_pairs={{0,3},{1,2},{2,1},{3,0},{4,7},{5,6},{6,5},{7,4},{8,11},{9,10},{10,... | collective-permute-start | bytes 1179656 | tf_op jit(solution)/shard_map/ppermute | solution.py:97
  72.9 48.8 %collective-permute-start.4 = (bf16[4,1,128,384]{3,2,1,0:T(8,128)(2,1)}, bf16[4,1,128,384]{3,2,1,0:T(8,128)(2,1)}, u32[]{:S(2)}, u32[]{:S(2)}) collective-permute-start(bf16[4,1,128,384]{3,2,1,0:T(8,128)(2,1)} %get-tuple-element.24), channel_id=1, source_target_pairs={{0,4},{1,5},{2,6},{3,7},{4,0},{5,1},{6,2},{7,3},{8,12},{9,13},{10,... | collective-permute-start | bytes 1179656 | tf_op jit(solution)/shard_map/ppermute | solution.py:97
  75.6 47.2 %collective-permute-start.5 = (bf16[4,1,128,384]{3,2,1,0:T(8,128)(2,1)}, bf16[4,1,128,384]{3,2,1,0:T(8,128)(2,1)}, u32[]{:S(2)}, u32[]{:S(2)}) collective-permute-start(bf16[4,1,128,384]{3,2,1,0:T(8,128)(2,1)} %get-tuple-element.17), channel_id=1, source_target_pairs={{0,5},{1,4},{2,7},{3,6},{4,1},{5,0},{6,3},{7,2},{8,13},{9,12},{10,... | collective-permute-start | bytes 1179656 | tf_op jit(solution)/shard_map/ppermute | solution.py:97
  76.2 34.8 %all-to-all-start = ((s32[4,8,128]{2,0,1:T(4,128)}), s32[4,8,128]{2,0,1:T(4,128)S(1)}, u32[]{:S(2)}, u32[]{:S(2)}) async-start(s32[4,8,128]{2,0,1:T(4,128)} %copy.73), calls=%async_computation | async-start | bytes 32768 | tf_op jit(solution)/shard_map/all_to_all | solution.py:100
  111.5 14.1 %collective-permute-start.6 = (bf16[4,1,128,384]{3,2,1,0:T(8,128)(2,1)}, bf16[4,1,128,384]{3,2,1,0:T(8,128)(2,1)S(1)}, u32[]{:S(2)}, u32[]{:S(2)}) collective-permute-start(bf16[4,1,128,384]{3,2,1,0:T(8,128)(2,1)} %get-tuple-element.16), channel_id=1, source_target_pairs={{0,6},{1,7},{2,4},{3,5},{4,2},{5,3},{6,0},{7,1},{8,14},{9,15},{10,... | collective-permute-start | bytes 1179656 | tf_op jit(solution)/shard_map/ppermute | solution.py:97
  116.3 17.2 %collective-permute-start.7 = (bf16[4,1,128,384]{3,2,1,0:T(8,128)(2,1)}, bf16[4,1,128,384]{3,2,1,0:T(8,128)(2,1)S(1)}, u32[]{:S(2)}, u32[]{:S(2)}) collective-permute-start(bf16[4,1,128,384]{3,2,1,0:T(8,128)(2,1)} %get-tuple-element.15), channel_id=1, source_target_pairs={{0,7},{1,6},{2,5},{3,4},{4,3},{5,2},{6,1},{7,0},{8,15},{9,14},{10,... | collective-permute-start | bytes 1179656 | tf_op jit(solution)/shard_map/ppermute | solution.py:97
  117.5 45.0 %collective-permute-start = (bf16[2,512,512]{1,2,0:T(8,128)(2,1)}, bf16[2,512,512]{1,2,0:T(8,128)(2,1)}, u32[]{:S(2)}, u32[]{:S(2)}) collective-permute-start(bf16[2,512,512]{1,2,0:T(8,128)(2,1)} %copy.92), channel_id=1, source_target_pairs={{0,1},{1,2},{2,3},{3,4},{4,5},{5,6},{6,7},{8,9},{9,10},{10,11},{11... | collective-permute-start | bytes 3145736 | tf_op jit(solution)/shard_map/ppermute | solution.py:15
  134.2 1.7 copy-start.2
  141.5 21.0 %copy-start.1 = (bf16[2,512,512]{1,2,0:T(8,128)(2,1)S(1)}, bf16[2,512,512]{1,2,0:T(8,128)(2,1)}, u32[]{:S(2)}) copy-start(bf16[2,512,512]{1,2,0:T(8,128)(2,1)} %copy.92) | copy-start | bytes 3145732
  142.9 45.9 %all-to-all-start.1 = ((bf16[4,8,128,128]{3,2,0,1:T(8,128)(2,1)}), bf16[4,8,128,128]{3,2,0,1:T(8,128)(2,1)S(1)}, u32[]{:S(2)}, u32[]{:S(2)}) async-start(bf16[4,8,128,128]{3,2,0,1:T(8,128)(2,1)} %copy.85), calls=%async_computation.1 | async-start | bytes 2097152 | tf_op jit(solution)/shard_map/all_to_all | solution.py:127
  162.3 98.9 %reduce-scatter.2.cloned.1.call-start = ((), (), s32[]{:S(2)}) async-start(), calls=%async_computation.3 | async-start | bytes 5242880 | tf_op jit(solution)/shard_map/reduce_scatter | solution.py:138
  173.0 4.6 %copy-start = (bf16[512,4096]{1,0:T(8,128)(2,1)S(1)}, bf16[512,4096]{1,0:T(8,128)(2,1)}, u32[]{:S(2)}) copy-start(bf16[512,4096]{1,0:T(8,128)(2,1)} %param.8) | copy-start | bytes 12582916
Sparse Core Ops, SparseCore 0:
  209.6 51.5 reduce-scatter.1
